TPU v7x, 128 devices: a whole 4x4x4 slice. The times are simulated.
128 devices in a mesh: req: 32 (over z, y, core), head: 4 (over x).
Axes of the slice: x: 4, y: 4, z: 4, core: 2. Of those that a mesh axis runs over, the one named last changes fastest.
Arguments:
- hidden_in: bfloat16 [512, 2048], P(None, 'req'), may hold values from -6 to 6
- lengths: int32 [512], P('req'), may hold values from 16 to 3072, as said below
- w_qkv: bfloat16 [3, 2048, 2048], P(None, 'req', 'head'), may hold values from -4 to 4, as said below
- qk_gain: float32 [2, 2048], P(None, 'head'), may hold values from 0.25 to 1.75
- cache_keys: bfloat16 [131072, 2048], P('req', 'head'), may hold values from -240 to 240
- cache_values: bfloat16 [131072, 2048], P('req', 'head'), may hold values from -6 to 6
- w_out: bfloat16 [2048, 2048], P('req', 'head'), may hold values from -3 to 3, as said below
- norm_gain: float32 [2, 2048], P(None, 'req'), may hold values from 0.25 to 1.75
- w_gate_up: bfloat16 [2, 2048, 8192], P(None, 'req', 'head'), may hold values from -0.125 to 0.125
- w_down: bfloat16 [2048, 8192], P('req', 'head'), may hold values from -3 to 3, as said below
Outputs:
- hidden_out: bfloat16 [512, 2048], P(None, 'req')
- new_keys: bfloat16 [512, 2048], P('req', 'head')
- new_values: bfloat16 [512, 2048], P('req', 'head')
Inputs may be any that keep to these rules, and one draw needn't show every extreme that they name: `lengths`: in each aligned group of requests 8 * 16 * k to 8 * 16 * k + 8 * 16 - 1 exactly one request, at a place drawn from the seed, has length 3072; every other length lies between 16 and 64. `w_qkv`: entries have magnitude at most 26 / sqrt(2048). `w_out`: entries have magnitude at most 23 / sqrt(2048). `w_down`: entries have magnitude at most 23 / sqrt(8192).
All inputs are finite; a program needn't handle non-finite values.
Results may differ from a plain program's by a relative error of at most 0.015.
Values may be sent and summed in bfloat16 or wider, within the bound.
No kernel may reach another device: no remote copies, remote signals or barrier semaphores. Data moves between devices by JAX's collectives and lax.ppermute only.
A program may use at most 128 MiB of HBM per device.

v0:
```python
import jax
import jax.numpy as jnp
from jax import lax
from jax.sharding import PartitionSpec as P

HEAD_DIM = 128
EPS = 1e-06
THETA = 500000.0


def rotate(values, positions):
    half = values.shape[-1] // 2
    freqs = jnp.power(THETA, -(jnp.arange(half, dtype=jnp.float32) * 2.0 / values.shape[-1]))
    angles = positions.astype(jnp.float32)[:, None] * freqs[None, :]
    cosine = jnp.cos(angles)[:, None, :]
    sine = jnp.sin(angles)[:, None, :]
    first = values[..., :half]
    second = values[..., half:]
    return jnp.concatenate(
        [first * cosine - second * sine, second * cosine + first * sine], axis=-1
    )


def contract_last(left, right):
    return lax.dot_general(
        left, right, (((1,), (1,)), ((), ())), preferred_element_type=jnp.float32
    )


def body(
    hidden_in,
    lengths,
    w_qkv,
    qk_gain,
    cache_keys,
    cache_values,
    w_out,
    norm_gain,
    w_gate_up,
    w_down,
):
    rows_here = lengths.shape[0]
    width_here = w_qkv.shape[2]
    heads_here = width_here // HEAD_DIM
    units_here = w_gate_up.shape[2]
    full_width = width_here * lax.axis_size("head")
    model_width = hidden_in.shape[1] * lax.axis_size("req")
    selected = hidden_in
    product = jnp.einsum("bd,gdf->bgf", selected, w_qkv, preferred_element_type=jnp.float32)
    projected = lax.psum_scatter(
        product.reshape(rows_here * lax.axis_size("req"), 3 * width_here),
        "req",
        scatter_dimension=0,
        tiled=True,
    )
    query = projected[:, :width_here]
    key_new = projected[:, width_here : 2 * width_here]
    value_new = projected[:, 2 * width_here :].astype(jnp.bfloat16)
    query_squares, key_squares = lax.psum(
        (jnp.sum(query * query, axis=1), jnp.sum(key_new * key_new, axis=1)), "head"
    )
    query = query * lax.rsqrt(query_squares[:, None] / full_width + EPS) * qk_gain[0]
    key_new = key_new * lax.rsqrt(key_squares[:, None] / full_width + EPS) * qk_gain[1]
    query_rot = rotate(query.reshape(rows_here, heads_here, HEAD_DIM), lengths).astype(jnp.bfloat16)
    key_rot = rotate(key_new.reshape(rows_here, heads_here, HEAD_DIM), lengths).astype(jnp.bfloat16)
    value_heads = value_new.reshape(rows_here, heads_here, HEAD_DIM)
    scale = HEAD_DIM ** (-0.5)
    starts = jnp.cumsum(lengths) - lengths
    ends = starts + lengths
    own_score = jnp.sum(query_rot.astype(jnp.float32) * key_rot.astype(jnp.float32), axis=2) * scale
    pool_rows = cache_keys.shape[0]
    block = 512

    def attend_block(index, carry):
        running_max, running_total, running_sum = carry
        offset = index * block
        block_keys = lax.dynamic_slice_in_dim(cache_keys, offset, block, 0).reshape(
            block, heads_here, HEAD_DIM
        )
        block_values = lax.dynamic_slice_in_dim(cache_values, offset, block, 0).reshape(
            block, heads_here, HEAD_DIM
        )
        scores = (
            jnp.einsum("rhd,phd->rhp", query_rot, block_keys, preferred_element_type=jnp.float32)
            * scale
        )
        positions = offset + jnp.arange(block, dtype=jnp.int32)
        inside = (positions[None, :] >= starts[:, None]) & (positions[None, :] < ends[:, None])
        scores = jnp.where(inside[:, None, :], scores, -jnp.inf)
        new_max = jnp.maximum(running_max, jnp.max(scores, axis=2))
        weights = jnp.exp(scores - new_max[:, :, None]).astype(jnp.bfloat16)
        factor = jnp.exp(running_max - new_max)
        running_total = running_total * factor + jnp.sum(weights.astype(jnp.float32), axis=2)
        running_sum = running_sum * factor[:, :, None] + jnp.einsum(
            "rhp,phd->rhd", weights, block_values, preferred_element_type=jnp.float32
        )
        return (new_max, running_total, running_sum)

    steps_count = pool_rows // block
    initial = (own_score, jnp.ones_like(own_score), value_heads.astype(jnp.float32))
    final_max, final_total, final_sum = lax.fori_loop(0, steps_count, attend_block, initial)
    attended = (
        (final_sum / final_total[:, :, None]).astype(jnp.bfloat16).reshape(rows_here, width_here)
    )
    attn_part = contract_last(lax.all_gather(attended, "req", axis=0, tiled=True), w_out)
    attn_full = lax.psum(attn_part, "head")
    attn_power = lax.psum(jnp.sum(attn_full * attn_full, axis=1), "req")
    attn_normed = attn_full * lax.rsqrt(attn_power[:, None] / model_width + EPS) * norm_gain[0]
    hidden_mid = (hidden_in.astype(jnp.float32) + attn_normed).astype(jnp.bfloat16)
    selected = hidden_mid
    product = jnp.einsum("bd,gdf->bgf", selected, w_gate_up, preferred_element_type=jnp.float32)
    combined = lax.psum_scatter(
        product.reshape(rows_here * lax.axis_size("req"), 2 * units_here),
        "req",
        scatter_dimension=0,
        tiled=True,
    )
    gated = combined[:, :units_here]
    lifted = combined[:, units_here:]
    activated = (jax.nn.silu(gated) * lifted).astype(jnp.bfloat16)
    down_part = contract_last(lax.all_gather(activated, "req", axis=0, tiled=True), w_down)
    ffn_full = lax.psum(down_part, "head")
    ffn_power = lax.psum(jnp.sum(ffn_full * ffn_full, axis=1), "req")
    ffn_normed = ffn_full * lax.rsqrt(ffn_power[:, None] / model_width + EPS) * norm_gain[1]
    hidden_out = (hidden_mid.astype(jnp.float32) + ffn_normed).astype(jnp.bfloat16)
    return (hidden_out, key_rot.reshape(rows_here, width_here), value_new)


def solution(mesh):
    return jax.shard_map(
        body,
        mesh=mesh,
        in_specs=(
            P(None, "req"),
            P("req"),
            P(None, "req", "head"),
            P(None, "head"),
            P("req", "head"),
            P("req", "head"),
            P("req", "head"),
            P(None, "req"),
            P(None, "req", "head"),
            P("req", "head"),
        ),
        out_specs=(P(None, "req"), P("req", "head"), P("req", "head")),
        check_vma=False,
    )
```

profile of v0, /device:TPU:0, one launch (start us, length us, event | category | flops | bytes accessed | tf_op | source)
XLA Modules:
  0.0 528.0 jit_solution(12049688516893260932)
XLA Ops:
  7.2 3.3 fusion.7
  10.6 3.6 copy.52
  14.6 82.7 %reduce-scatter.5.cloned.1.call-done = f32[16,1536]{1,0:T(8,128)} async-done(((f32[512,1536]{1,0:T(8,128)}), f32[16,1536]{1,0:T(8,128)}) %reduce-scatter.5.cloned.1.call-update) | async-done | bytes 98320 | tf_op jit(solution)/shard_map/reduce_scatter | solution.py:50
  97.3 0.9 multiply_reduce_fusion.4
  98.2 10.5 %all-reduce = (f32[16]{0:T(128)S(1)}, f32[16]{0:T(128)S(1)}) all-reduce(f32[16]{0:T(128)S(1)} %get-tuple-element.227, f32[16]{0:T(128)S(1)} %get-tuple-element.226), channel_id=1, replica_groups=mesh['req'=32,'head'=4] {'head'}, use_global_device_ids=true, to_apply=%region_4.0 | all-reduce | flops 32 | bytes 256 | tf_op jit(solution)/shard_map/psum | solution.py:59
  108.7 0.9 multiply_multiply_fusion
  109.5 1.4 convert_bitcast_fusion
  111.3 20.6 %while.18 = (s32[]{:T(128)}, f32[16,4]{0,1:T(4,128)S(1)}, f32[16,4]{0,1:T(4,128)S(1)}, f32[16,4,128]{2,0,1:T(8,128)S(1)}, s32[16]{0:T(128)S(1)}, /*index=5*/s32[...) while((s32[]{:T(128)}, f32[16,4]{0,1:T(4,128)S(1)}, ...), condition=%wide.region_10.11_spmd.clone, body=%wide.region_7.10_spmd.clone.sunk | while | flops 17113800 | bytes 5742917 | solution.py:101
  111.4 1.3 constant_dynamic-slice_fusion.3
  114.0 1.3 constant_dynamic-slice_fusion.3
  116.6 1.3 constant_dynamic-slice_fusion.3
  119.2 1.3 constant_dynamic-slice_fusion.3
  121.8 1.3 constant_dynamic-slice_fusion.3
  124.3 1.3 constant_dynamic-slice_fusion.3
  126.9 1.3 constant_dynamic-slice_fusion.3
  129.5 1.3 constant_dynamic-slice_fusion.3
  132.1 24.1 %all_gather.6 = bf16[512,512]{1,0:T(8,128)(2,1)S(1)} all-gather(bf16[16,512]{1,0:T(8,128)(2,1)S(1)} %copy_bitcast_fusion.2), channel_id=1, replica_groups=mesh['req'=32,'head'=4] {'req'}, dimensions={0}, use_global_device_ids=true | all-gather | bytes 540672 | tf_op jit(solution)/shard_map/all_gather | solution.py:105
  156.2 0.9 fusion.15
  157.3 37.5 %all-reduce.4.cloned.1.call-done = f32[512,64]{0,1:T(8,128)} async-done(((f32[512,64]{0,1:T(8,128)}), f32[512,64]{0,1:T(8,128)}) %all-reduce.4.cloned.1.call-update) | async-done | bytes 131088 | tf_op jit(solution)/shard_map/psum | solution.py:106
  194.8 0.9 multiply_reduce_fusion.1
  195.7 65.2 %psum.45 = f32[512]{0:T(512)S(1)} all-reduce(f32[512]{0:T(512)S(1)} %multiply_reduce_fusion.1), channel_id=1, replica_groups=mesh['req'=32,'head'=4] {'req'}, use_global_device_ids=true, to_apply=%region_13.14 | all-reduce | flops 512 | bytes 4096 | tf_op jit(solution)/shard_map/psum | solution.py:107
  260.9 1.0 add_convert_fusion.1
  261.9 4.5 fusion.5
  266.4 8.9 %copy.69 = f32[512,4096]{1,0:T(8,128)} copy(f32[512,4096]{0,1:T(8,128)} %bitcast.64) | data formatting | bytes 16777216
  275.4 88.6 %reduce-scatter.7.cloned.1.call-done = f32[16,4096]{1,0:T(8,128)} async-done(((f32[512,4096]{1,0:T(8,128)}), f32[16,4096]{1,0:T(8,128)}) %reduce-scatter.7.cloned.1.call-update) | async-done | bytes 262160 | tf_op jit(solution)/shard_map/reduce_scatter | solution.py:112
  364.0 1.6 fusion.4
  365.7 44.5 %all-gather.2.cloned.1.call-done = bf16[512,2048]{1,0:T(8,128)(2,1)} async-done(((bf16[16,2048]{1,0:T(8,128)(2,1)}), bf16[512,2048]{1,0:T(8,128)(2,1)}) %all-gather.2.cloned.1.call-update) | async-done | bytes 2097168 | tf_op jit(solution)/shard_map/all_gather | solution.py:121
  410.2 3.0 fusion.16
  413.9 39.9 %all-reduce.6.cloned.1.call-done = f32[512,64]{0,1:T(8,128)} async-done(((f32[512,64]{0,1:T(8,128)}), f32[512,64]{0,1:T(8,128)}) %all-reduce.6.cloned.1.call-update) | async-done | bytes 131088 | tf_op jit(solution)/shard_map/psum | solution.py:122
  453.7 0.9 multiply_reduce_fusion
  454.7 65.2 %psum.47 = f32[512]{0:T(512)S(1)} all-reduce(f32[512]{0:T(512)S(1)} %multiply_reduce_fusion), channel_id=1, replica_groups=mesh['req'=32,'head'=4] {'req'}, use_global_device_ids=true, to_apply=%region_17.18 | all-reduce | flops 512 | bytes 4096 | tf_op jit(solution)/shard_map/psum | solution.py:123
  519.8 1.6 add_convert_fusion
  (127 shorter events, 11.9 us)
Async XLA Ops:
  7.2 254.7 %copy-start = (bf16[2,64,2048]{2,1,0:T(8,128)(2,1)S(1)}, bf16[2,64,2048]{2,1,0:T(8,128)(2,1)}, u32[]{:S(2)}) copy-start(bf16[2,64,2048]{2,1,0:T(8,128)(2,1)} %param.20) | copy-start | bytes 1572868
  7.2 90.1 %reduce-scatter.5.cloned.1.call-start = ((), (), s32[]{:S(2)}) async-start(), calls=%async_computation.2 | async-start | bytes 3244032 | tf_op jit(solution)/shard_map/reduce_scatter | solution.py:50
  10.6 3.7 copy-start.5
  10.6 3.9 copy-start.4
  14.2 180.6 %all-reduce.4.cloned.1.call-start = ((), (), s32[]{:S(2)}) async-start(), calls=%async_computation.3 | async-start | bytes 262144 | tf_op jit(solution)/shard_map/psum | solution.py:106
  111.3 44.9 %copy-start.3 = (bf16[64,512]{1,0:T(8,128)(2,1)S(1)}, bf16[64,512]{1,0:T(8,128)(2,1)}, u32[]{:S(2)}) copy-start(bf16[64,512]{1,0:T(8,128)(2,1)} %param.18) | copy-start | bytes 196612
  111.3 45.9 %copy-start.6 = (f32[2,64]{1,0:T(2,128)S(1)}, f32[2,64]{1,0:T(2,128)}, u32[]{:S(2)}) copy-start(f32[2,64]{1,0:T(2,128)} %param.19) | copy-start | bytes 1540
  111.3 149.6 %copy-start.2 = (bf16[512,64]{0,1:T(8,128)(2,1)S(1)}, bf16[512,64]{0,1:T(8,128)(2,1)}, u32[]{:S(2)}) copy-start(bf16[512,64]{0,1:T(8,128)(2,1)} %param.12) | copy-start | bytes 196612
  157.2 206.8 %reduce-scatter.7.cloned.1.call-start = ((), (), s32[]{:S(2)}) async-start(), calls=%async_computation.6 | async-start | bytes 8650752 | tf_op jit(solution)/shard_map/reduce_scatter | solution.py:112
  275.3 134.9 %copy-start.1 = (bf16[64,2048]{1,0:T(8,128)(2,1)S(1)}, bf16[64,2048]{1,0:T(8,128)(2,1)}, u32[]{:S(2)}) copy-start(bf16[64,2048]{1,0:T(8,128)(2,1)} %param.21) | copy-start | bytes 786436
  275.4 134.9 %all-gather.2.cloned.1.call-start = ((), (), s32[]{:S(2)}) async-start(), calls=%async_computation.4 | async-start | bytes 2162688 | tf_op jit(solution)/shard_map/all_gather | solution.py:121
  365.7 88.1 %all-reduce.6.cloned.1.call-start = ((), (), s32[]{:S(2)}) async-start(), calls=%async_computation.5 | async-start | bytes 262144 | tf_op jit(solution)/shard_map/psum | solution.py:122
Sparse Core Ops, SparseCore 0:
  14.3 82.9 reduce-scatter.4
  157.3 37.4 all-reduce.3
  275.5 88.4 reduce-scatter.6
  367.0 43.2 all-gather.1
  413.4 40.3 all-reduce.5
where the time goes:
time: 529 us; the launch traced here: 528 us
  waiting for transfers between devices  293 us (55%)
  blocking collectives  165 us (31%)
  local copies, waits for them, and re-layouts  27.1 us (5%)
  matrix products  16.1 us (3%)
  between operations  13.9 us (3%)
  other arithmetic  12.2 us (2%)
    reduce_scatter x1, waiting for transfers between devices, body(): lax.psum_scatter(product.reshape(rows_here * lax.axis_size('req'), 2 * un...  88.6 us
    reduce_scatter x1, waiting for transfers between devices, body(): lax.psum_scatter(product.reshape(rows_here * lax.axis_size('req'), 3 * wi...  82.7 us
    psum x1, blocking collectives, body(): attn_power = lax.psum(jnp.sum(attn_full * attn_full, axis=1), 'req')  65.2 us
    psum x1, blocking collectives, body(): ffn_power = lax.psum(jnp.sum(ffn_full * ffn_full, axis=1), 'req')  65.2 us
    all_gather x1, waiting for transfers between devices, body(): lax.all_gather(activated, 'req', axis=0, tiled=True)  44.5 us
    psum x1, waiting for transfers between devices, body(): ffn_full = lax.psum(down_part, 'head')  39.9 us
    psum x1, waiting for transfers between devices, body(): attn_full = lax.psum(attn_part, 'head')  37.5 us
    all_gather x1, blocking collectives, body(): lax.all_gather(attended, 'req', axis=0, tiled=True)  24.1 us
  transfers between devices with their start and end apart: 5, of which 5 were waited for; matrix products, arithmetic and copies ran while one was open for 0% of the time, Pallas kernels for 0%

commit v1 on v0

--- a/solution.py
+++ b/solution.py
@@ -6,6 +6,11 @@
 HEAD_DIM = 128
 EPS = 1e-06
 THETA = 500000.0
+
+
+def gather_by_exchange(x, axis, dim):
+    copies = jnp.concatenate([x] * lax.axis_size(axis), axis=dim)
+    return lax.all_to_all(copies, axis, dim, dim, tiled=True)
 
 
 def rotate(values, positions):
@@ -102,7 +107,7 @@
     attended = (
         (final_sum / final_total[:, :, None]).astype(jnp.bfloat16).reshape(rows_here, width_here)
     )
-    attn_part = contract_last(lax.all_gather(attended, "req", axis=0, tiled=True), w_out)
+    attn_part = contract_last(gather_by_exchange(attended, "req", 0), w_out)
     attn_full = lax.psum(attn_part, "head")
     attn_power = lax.psum(jnp.sum(attn_full * attn_full, axis=1), "req")
     attn_normed = attn_full * lax.rsqrt(attn_power[:, None] / model_width + EPS) * norm_gain[0]

time: 529 us -> 523 us (0.989)
  blocking collectives: 165 us -> 157 us
    all_gather x1 -> x0, blocking collectives: 24.1 us -> none  [body(): lax.all_gather(attended, 'req', axis=0, tiled=True)]
    all_to_all x0 -> x1, blocking collectives: none -> 16.7 us  [gather_by_exchange(): return lax.all_to_all(copies, axis, dim, dim, tiled=True)]
where the time goes in v1:
time: 523 us; the launch traced here: 522 us
  waiting for transfers between devices  292 us (56%)
  blocking collectives  157 us (30%)
  local copies, waits for them, and re-layouts  27.1 us (5%)
  matrix products  16.1 us (3%)
  other arithmetic  14.7 us (3%)
  between operations  14.1 us (3%)
    reduce_scatter x1, waiting for transfers between devices, body(): lax.psum_scatter(product.reshape(rows_here * lax.axis_size('req'), 2 * un...  88.6 us
    reduce_scatter x1, waiting for transfers between devices, body(): lax.psum_scatter(product.reshape(rows_here * lax.axis_size('req'), 3 * wi...  82.7 us
    psum x1, blocking collectives, body(): ffn_power = lax.psum(jnp.sum(ffn_full * ffn_full, axis=1), 'req')  65.2 us
    psum x1, blocking collectives, body(): attn_power = lax.psum(jnp.sum(attn_full * attn_full, axis=1), 'req')  65.2 us
    all_gather x1, waiting for transfers between devices, body(): lax.all_gather(activated, 'req', axis=0, tiled=True)  44.5 us
    psum x1, waiting for transfers between devices, body(): ffn_full = lax.psum(down_part, 'head')  39.9 us
    psum x1, waiting for transfers between devices, body(): attn_full = lax.psum(attn_part, 'head')  36.7 us
    all_to_all x1, blocking collectives, gather_by_exchange(): return lax.all_to_all(copies, axis, dim, dim, tiled=True)  16.7 us
  transfers between devices with their start and end apart: 5, of which 5 were waited for; matrix products, arithmetic and copies ran while one was open for 0% of the time, Pallas kernels for 0%

profile of v1, /device:TPU:0, one launch (start us, length us, event | category | flops | bytes accessed | tf_op | source)
XLA Modules:
  0.0 522.5 jit_solution(6187824510059765378)
XLA Ops:
  7.2 3.3 fusion.7
  10.6 3.6 copy.52
  14.6 82.7 %reduce-scatter.5.cloned.1.call-done = f32[16,1536]{1,0:T(8,128)} async-done(((f32[512,1536]{1,0:T(8,128)}), f32[16,1536]{1,0:T(8,128)}) %reduce-scatter.5.cloned.1.call-update) | async-done | bytes 98320 | tf_op jit(solution)/shard_map/reduce_scatter | solution.py:55
  97.3 0.9 multiply_reduce_fusion.4
  98.2 10.5 %all-reduce = (f32[16]{0:T(128)S(1)}, f32[16]{0:T(128)S(1)}) all-reduce(f32[16]{0:T(128)S(1)} %get-tuple-element.227, f32[16]{0:T(128)S(1)} %get-tuple-element.226), channel_id=1, replica_groups=mesh['req'=32,'head'=4] {'head'}, use_global_device_ids=true, to_apply=%region_4.0 | all-reduce | flops 32 | bytes 256 | tf_op jit(solution)/shard_map/psum | solution.py:64
  108.7 0.9 multiply_multiply_fusion
  109.5 1.4 convert_bitcast_fusion
  111.3 20.7 %while.18 = (s32[]{:T(128)}, f32[16,4]{0,1:T(4,128)S(1)}, f32[16,4]{0,1:T(4,128)S(1)}, f32[16,4,128]{2,0,1:T(8,128)S(1)}, s32[16]{0:T(128)S(1)}, /*index=5*/s32[...) while((s32[]{:T(128)}, f32[16,4]{0,1:T(4,128)S(1)}, ...), condition=%wide.region_10.11_spmd.clone, body=%wide.region_7.10_spmd.clone.sunk | while | flops 17113800 | bytes 5742917 | solution.py:106
  111.4 1.3 constant_dynamic-slice_fusion.3
  114.0 1.3 constant_dynamic-slice_fusion.3
  116.6 1.3 constant_dynamic-slice_fusion.3
  119.2 1.3 constant_dynamic-slice_fusion.3
  121.8 1.3 constant_dynamic-slice_fusion.3
  124.4 1.3 constant_dynamic-slice_fusion.3
  126.9 1.3 constant_dynamic-slice_fusion.3
  129.5 1.3 constant_dynamic-slice_fusion.3
  134.8 16.7 %all_to_all.12 = bf16[32,16,512]{2,1,0:T(8,128)(2,1)S(1)} all-to-all(bf16[32,16,512]{2,1,0:T(8,128)(2,1)S(1)} %bitcast.132), channel_id=1, replica_groups=mesh['req'=32,'head'=4] {'req'}, dimensions={0} | all-to-all | bytes 1048576 | tf_op jit(solution)/shard_map/all_to_all | solution.py:13
  151.5 0.9 fusion.15
  152.6 36.7 %all-reduce.4.cloned.1.call-done = f32[512,64]{0,1:T(8,128)} async-done(((f32[512,64]{0,1:T(8,128)}), f32[512,64]{0,1:T(8,128)}) %all-reduce.4.cloned.1.call-update) | async-done | bytes 131088 | tf_op jit(solution)/shard_map/psum | solution.py:111
  189.2 0.9 multiply_reduce_fusion.1
  190.2 65.2 %psum.45 = f32[512]{0:T(512)S(1)} all-reduce(f32[512]{0:T(512)S(1)} %multiply_reduce_fusion.1), channel_id=1, replica_groups=mesh['req'=32,'head'=4] {'req'}, use_global_device_ids=true, to_apply=%region_13.14 | all-reduce | flops 512 | bytes 4096 | tf_op jit(solution)/shard_map/psum | solution.py:112
  255.3 1.0 add_convert_fusion.1
  256.3 4.5 fusion.5
  260.9 8.9 %copy.69 = f32[512,4096]{1,0:T(8,128)} copy(f32[512,4096]{0,1:T(8,128)} %bitcast.129) | data formatting | bytes 16777216
  269.9 88.6 %reduce-scatter.7.cloned.1.call-done = f32[16,4096]{1,0:T(8,128)} async-done(((f32[512,4096]{1,0:T(8,128)}), f32[16,4096]{1,0:T(8,128)}) %reduce-scatter.7.cloned.1.call-update) | async-done | bytes 262160 | tf_op jit(solution)/shard_map/reduce_scatter | solution.py:117
  358.5 1.6 fusion.4
  360.2 44.5 %all-gather.2.cloned.1.call-done = bf16[512,2048]{1,0:T(8,128)(2,1)} async-done(((bf16[16,2048]{1,0:T(8,128)(2,1)}), bf16[512,2048]{1,0:T(8,128)(2,1)}) %all-gather.2.cloned.1.call-update) | async-done | bytes 2097168 | tf_op jit(solution)/shard_map/all_gather | solution.py:126
  404.7 3.0 fusion.16
  408.4 39.9 %all-reduce.6.cloned.1.call-done = f32[512,64]{0,1:T(8,128)} async-done(((f32[512,64]{0,1:T(8,128)}), f32[512,64]{0,1:T(8,128)}) %all-reduce.6.cloned.1.call-update) | async-done | bytes 131088 | tf_op jit(solution)/shard_map/psum | solution.py:127
  448.2 0.9 multiply_reduce_fusion
  449.2 65.2 %psum.47 = f32[512]{0:T(512)S(1)} all-reduce(f32[512]{0:T(512)S(1)} %multiply_reduce_fusion), channel_id=1, replica_groups=mesh['req'=32,'head'=4] {'req'}, use_global_device_ids=true, to_apply=%region_17.18 | all-reduce | flops 512 | bytes 4096 | tf_op jit(solution)/shard_map/psum | solution.py:128
  514.3 1.6 add_convert_fusion
  (158 shorter events, 14.4 us)
Async XLA Ops:
  7.2 249.2 %copy-start = (bf16[2,64,2048]{2,1,0:T(8,128)(2,1)S(1)}, bf16[2,64,2048]{2,1,0:T(8,128)(2,1)}, u32[]{:S(2)}) copy-start(bf16[2,64,2048]{2,1,0:T(8,128)(2,1)} %param.20) | copy-start | bytes 1572868
  7.2 90.1 %reduce-scatter.5.cloned.1.call-start = ((), (), s32[]{:S(2)}) async-start(), calls=%async_computation.3 | async-start | bytes 3244032 | tf_op jit(solution)/shard_map/reduce_scatter | solution.py:55
  10.6 3.7 copy-start.5
  10.6 3.9 copy-start.4
  14.2 175.1 %all-reduce.4.cloned.1.call-start = ((), (), s32[]{:S(2)}) async-start(), calls=%async_computation.4 | async-start | bytes 262144 | tf_op jit(solution)/shard_map/psum | solution.py:111
  111.3 40.2 %copy-start.3 = (bf16[64,512]{1,0:T(8,128)(2,1)S(1)}, bf16[64,512]{1,0:T(8,128)(2,1)}, u32[]{:S(2)}) copy-start(bf16[64,512]{1,0:T(8,128)(2,1)} %param.18) | copy-start | bytes 196612
  111.3 41.2 %copy-start.6 = (f32[2,64]{1,0:T(2,128)S(1)}, f32[2,64]{1,0:T(2,128)}, u32[]{:S(2)}) copy-start(f32[2,64]{1,0:T(2,128)} %param.19) | copy-start | bytes 1540
  111.3 144.0 %copy-start.2 = (bf16[512,64]{0,1:T(8,128)(2,1)S(1)}, bf16[512,64]{0,1:T(8,128)(2,1)}, u32[]{:S(2)}) copy-start(bf16[512,64]{0,1:T(8,128)(2,1)} %param.12) | copy-start | bytes 196612
  152.5 206.0 %reduce-scatter.7.cloned.1.call-start = ((), (), s32[]{:S(2)}) async-start(), calls=%async_computation.7 | async-start | bytes 8650752 | tf_op jit(solution)/shard_map/reduce_scatter | solution.py:117
  269.8 134.9 %copy-start.1 = (bf16[64,2048]{1,0:T(8,128)(2,1)S(1)}, bf16[64,2048]{1,0:T(8,128)(2,1)}, u32[]{:S(2)}) copy-start(bf16[64,2048]{1,0:T(8,128)(2,1)} %param.21) | copy-start | bytes 786436
  269.8 134.9 %all-gather.2.cloned.1.call-start = ((), (), s32[]{:S(2)}) async-start(), calls=%async_computation.5 | async-start | bytes 2162688 | tf_op jit(solution)/shard_map/all_gather | solution.py:126
  360.1 88.1 %all-reduce.6.cloned.1.call-start = ((), (), s32[]{:S(2)}) async-start(), calls=%async_computation.6 | async-start | bytes 262144 | tf_op jit(solution)/shard_map/psum | solution.py:127
Sparse Core Ops, SparseCore 0:
  14.3 82.9 reduce-scatter.4
  152.6 36.5 all-reduce.3
  269.9 88.4 reduce-scatter.6
  361.4 43.2 all-gather.1
  407.9 40.3 all-reduce.5
